TPU v7x, 32 devices: a whole 2x2x4 slice. The times are simulated.
32 devices in a mesh: row: 2 (over x), col: 16 (over z, y, core).
Axes of the slice: x: 2, y: 2, z: 4, core: 2. Of those that a mesh axis runs over, the one named last changes fastest.
Arguments:
- query_proj: bfloat16 [16384, 4096], P(('col', 'row')), may hold values from -9 to 9
- key_proj: bfloat16 [16384, 512], P(('col', 'row')), may hold values from -9 to 9
- value_proj: bfloat16 [16384, 512], P(('col', 'row')), may hold values from -6 to 6
- segment_ids: int32 [16, 1024], P('col'), may hold values from 0 to 3, never falling along the last dimension, each value on 1 to 512 neighbouring positions
- out_weight: bfloat16 [4096, 8192], P('col', 'row'), may hold values from -0.09375 to 0.09375
- residual: bfloat16 [16384, 8192], P('col', 'row'), may hold values from -4 to 4
- norm_gain: float32 [8192], P('row'), may hold values from 0.1 to 1.9
Outputs:
- residual_sum: bfloat16 [16384, 8192], P('col', 'row')
- normed: bfloat16 [16384, 8192], P('col', 'row')
Inputs may be any that keep to these rules, and one draw needn't show every extreme that they name: `segment_ids`: along each packed sequence the document number never falls; each document spans at most 512 positions and one spans exactly that.
All inputs are finite; a program needn't handle non-finite values.
Results may differ from a plain program's by a relative error of at most 0.0044.
Values may be sent and summed in bfloat16 or wider, within the bound.
A program may use at most 192 MiB of HBM per device.

v0:
```python
import jax
import jax.numpy as jnp
from jax import lax
from jax.sharding import PartitionSpec as P

D = 8192
HD = 128
HK = 4


def attend_local(query_heads, key_heads, value_heads, segment_row):
    length = query_heads.shape[0]
    kv_local = key_heads.shape[1] // HD
    group = query_heads.shape[1] // HD // kv_local
    query_grid = query_heads.reshape(length, kv_local, group, HD).transpose(1, 2, 0, 3)
    key_grid = key_heads.reshape(length, kv_local, HD).transpose(1, 0, 2)
    value_grid = value_heads.reshape(length, kv_local, HD).transpose(1, 0, 2)
    places = jnp.arange(length)
    allowed = (segment_row[:, None] == segment_row[None, :]) & (places[None, :] <= places[:, None])

    def one_group(operands):
        group_query, group_key, group_value = operands
        scores = jnp.einsum(
            "gqd,kd->gqk", group_query, group_key, preferred_element_type=jnp.float32
        ) * HD ** (-0.5)
        scores = jnp.where(allowed, scores, jnp.float32(-1e30))
        peak = jnp.max(scores, axis=-1, keepdims=True)
        weights = jnp.where(allowed, jnp.exp(scores - peak), jnp.float32(0.0))
        totals = jnp.sum(weights, axis=-1, keepdims=True)
        probs = weights.astype(jnp.bfloat16)
        mixture = (
            jnp.einsum("gqk,kd->gqd", probs, group_value, preferred_element_type=jnp.float32)
            / totals
        )
        return mixture.astype(jnp.bfloat16)

    heads_out = lax.map(one_group, (query_grid, key_grid, value_grid))
    return heads_out.transpose(2, 0, 1, 3).reshape(length, kv_local * group * HD)


def widen_heads(proj_rows, repeat):
    rows_local = proj_rows.shape[0]
    kv_count = proj_rows.shape[1] // HD
    if repeat == 1:
        return proj_rows
    spread = jnp.broadcast_to(
        proj_rows.reshape(rows_local, kv_count, 1, HD), (rows_local, kv_count, repeat, HD)
    )
    return spread.reshape(rows_local, kv_count * repeat * HD)


def body(query_proj, key_proj, value_proj, segment_ids, out_weight, residual, norm_gain):
    row_count = lax.axis_size("row")
    repeat = max(row_count // HK, 1)
    key_wide = widen_heads(key_proj, repeat)
    value_wide = widen_heads(value_proj, repeat)
    query_heads, key_heads, value_heads = (
        lax.all_to_all(query_proj, "row", split_axis=1, concat_axis=0, tiled=True),
        lax.all_to_all(key_wide, "row", split_axis=1, concat_axis=0, tiled=True),
        lax.all_to_all(value_wide, "row", split_axis=1, concat_axis=0, tiled=True),
    )
    attn = attend_local(query_heads, key_heads, value_heads, segment_ids[0])
    panel_rows = lax.all_gather(attn, "row", axis=1, tiled=True)
    projected = jnp.dot(
        panel_rows,
        lax.all_gather(out_weight, "col", axis=0, tiled=True),
        preferred_element_type=jnp.float32,
    )
    hidden_sum = residual.astype(jnp.float32) + projected
    squares = lax.psum(jnp.sum(hidden_sum * hidden_sum, axis=1), "row")
    scaled = lax.rsqrt(squares / D + jnp.float32(1e-05))
    normed = hidden_sum * scaled[:, None] * norm_gain[None, :]
    return (hidden_sum.astype(jnp.bfloat16), normed.astype(jnp.bfloat16))


def solution(mesh):
    placed = (
        P(("col", "row"), None),
        P(("col", "row"), None),
        P(("col", "row"), None),
        P("col", None),
        P("col", "row"),
        P("col", "row"),
        P("row"),
    )
    return jax.shard_map(
        body,
        mesh=mesh,
        in_specs=placed,
        out_specs=(P("col", "row"), P("col", "row")),
        check_vma=False,
    )
```

profile of v0, /device:TPU:1, one launch (start us, length us, event | category | flops | bytes accessed | tf_op | source)
XLA Modules:
  0.0 513.6 jit_solution(6233350073334996084)
XLA Ops:
  7.2 1.9 copy.42
  9.0 3.5 all-to-all-start.1
  12.5 1.9 copy.41
  14.4 6.4 %all-to-all-done.1 = bf16[512,2,256]{2,0,1:T(8,128)(2,1)S(1)} async-done(((bf16[512,2,256]{2,0,1:T(8,128)(2,1)}), bf16[512,2,256]{2,0,1:T(8,128)(2,1)S(1)}, u32[]{:S(2)}, u32[]{:S(2)}) %all-to-all-start.1) | async-done | bytes 524320 | tf_op jit(solution)/shard_map/all_to_all | solution.py:59
  20.8 3.5 all-to-all-start.2
  24.3 4.8 copy.40
  29.1 2.0 all-to-all-done.2
  31.1 5.6 %all-to-all-start = ((bf16[512,2,2048]{2,0,1:T(8,128)(2,1)}), bf16[512,2,2048]{2,0,1:T(8,128)(2,1)}, u32[]{:S(2)}, u32[]{:S(2)}) async-start(bf16[512,2,2048]{2,0,1:T(8,128)(2,1)} %bitcast.71), calls=%async_computation | async-start | bytes 8388608 | tf_op jit(solution)/shard_map/all_to_all | solution.py:58
  36.8 0.1 reshape.34
  36.9 0.9 copy.15
  37.9 0.9 copy.16
  38.8 43.2 %all-to-all-done = bf16[512,2,2048]{2,0,1:T(8,128)(2,1)} async-done(((bf16[512,2,2048]{2,0,1:T(8,128)(2,1)}), bf16[512,2,2048]{2,0,1:T(8,128)(2,1)}, u32[]{:S(2)}, u32[]{:S(2)}) %all-to-all-start) | async-done | bytes 4194336 | tf_op jit(solution)/shard_map/all_to_all | solution.py:58
  82.0 5.6 %copy.25 = bf16[128,8,16,128]{3,2,1,0:T(8,128)(2,1)} copy(bf16[128,8,16,128]{3,1,2,0:T(8,128)(2,1)} %bitcast.23) | data formatting | bytes 8388608
  87.6 74.1 %while.11 = (s32[]{:T(128)}, bf16[2,8,1024,128]{2,3,1,0:T(8,128)(2,1)}, bf16[2,8,1024,128]{3,1,0,2:T(8,128)(2,1)}, bf16[2,1024,128]{2,1,0:T(8,128)(2,1)}, bf16[2...) while((s32[]{:T(128)}, bf16[2,8,1024,128]{2,3,1,0:T(8,128)(2,1)}, ...), condition=%wide.region_3.4_spmd.clone, body=%wide.region_0.3_spmd.clone.sunk | while | flops 4350542848 | bytes 54072912 | solution.py:37
  87.6 1.7 constant_dynamic-slice_fusion.2
  89.3 0.6 fusion.52
  89.9 20.1 %fusion.53 = (f32[8,1024]{1,0:T(8,128)S(1)}, bf16[8,1024,1024]{1,2,0:T(8,128)(2,1)}) fusion(pred[1024,1024]{0,1:T(8,128)(4,1)S(1)} %fusion.52, bf16[1,8,1024,128]{3,1,0,2:T(8,128)(2,1)S(1)} %constant_dynamic-slice_fusion.2, bf16[2,1024,128]{2,1,0:T(8,128)(2,1)} %get-tuple-element.134, s32[]{:T(128)} %get-tuple-element.124), kind=kOutput, calls=%fused_computation.37.clone.1 | convolution fusion | flops 2197816320 | bytes 21266944 | tf_op jit(solution)/shard_map/while/body/eval_jaxpr/sub | solution.py:28
  110.0 10.1 %fusion.54 = bf16[1,8,1024,128]{3,2,1,0:T(8,128)(2,1)} fusion(f32[8,1024]{1,0:T(8,128)S(1)} %get-tuple-element.115, bf16[8,1024,1024]{1,2,0:T(8,128)(2,1)} %get-tuple-element.116, bf16[2,1024,128]{2,1,0:T(8,128)(2,1)} %get-tuple-element.135, s32[]{:T(128)} %get-tuple-element.124), kind=kOutput, calls=%fused_computation.16.clone.1 | convolution fusion | flops 2149580800 | bytes 19169792 | tf_op jit(solution)/shard_map/while/body/eval_jaxpr/gqk,kd->gqd/dot_general | solution.py:32
  120.1 2.9 copy.46
  123.0 1.6 constant_dynamic-update-slice_fusion.2
  124.6 1.7 constant_dynamic-slice_fusion.2
  126.4 0.6 fusion.52
  127.0 20.1 %fusion.53 = (f32[8,1024]{1,0:T(8,128)S(1)}, bf16[8,1024,1024]{1,2,0:T(8,128)(2,1)}) fusion(pred[1024,1024]{0,1:T(8,128)(4,1)S(1)} %fusion.52, bf16[1,8,1024,128]{3,1,0,2:T(8,128)(2,1)S(1)} %constant_dynamic-slice_fusion.2, bf16[2,1024,128]{2,1,0:T(8,128)(2,1)} %get-tuple-element.134, s32[]{:T(128)} %get-tuple-element.124), kind=kOutput, calls=%fused_computation.37.clone.1 | convolution fusion | flops 2197816320 | bytes 21266944 | tf_op jit(solution)/shard_map/while/body/eval_jaxpr/sub | solution.py:28
  147.1 10.1 %fusion.54 = bf16[1,8,1024,128]{3,2,1,0:T(8,128)(2,1)} fusion(f32[8,1024]{1,0:T(8,128)S(1)} %get-tuple-element.115, bf16[8,1024,1024]{1,2,0:T(8,128)(2,1)} %get-tuple-element.116, bf16[2,1024,128]{2,1,0:T(8,128)(2,1)} %get-tuple-element.135, s32[]{:T(128)} %get-tuple-element.124), kind=kOutput, calls=%fused_computation.16.clone.1 | convolution fusion | flops 2149580800 | bytes 19169792 | tf_op jit(solution)/shard_map/while/body/eval_jaxpr/gqk,kd->gqd/dot_general | solution.py:32
  157.2 2.9 copy.46
  160.1 1.6 constant_dynamic-update-slice_fusion.2
  161.8 0.7 all-gather.5.cloned.1.call-update
  162.5 105.7 %all-gather.3.cloned.1.call-done = bf16[1024,4096]{0,1:T(8,128)(2,1)} async-done(((bf16[1024,2048]{0,1:T(8,128)(2,1)}), bf16[1024,4096]{0,1:T(8,128)(2,1)}) %all-gather.3.cloned.1.call-update) | async-done | bytes 8388624 | tf_op jit(solution)/shard_map/all_gather | solution.py:63
  268.2 170.1 %all-gather.5.cloned.1.call-done = bf16[4096,4096]{1,0:T(8,128)(2,1)} async-done(((bf16[256,4096]{1,0:T(8,128)(2,1)}), bf16[4096,4096]{1,0:T(8,128)(2,1)}) %all-gather.5.cloned.1.call-update) | async-done | bytes 33554448 | tf_op jit(solution)/shard_map/all_gather | solution.py:66
  438.3 45.1 %multiply_reduce_fusion = (f32[1024]{0:T(1024)S(1)}, f32[1024,4096]{1,0:T(8,128)}) fusion(bf16[1024,4096]{0,1:T(8,128)(2,1)} %all-gather.3.cloned.1.call-done, bf16[4096,4096]{1,0:T(8,128)(2,1)} %all-gather.5.cloned.1.call-done, bf16[1024,4096]{1,0:T(8,128)(2,1)} %param.14), kind=kOutput, calls=%fused_computation.31 | convolution fusion | flops 34376515584 | bytes 67112960 | tf_op jit(solution)/shard_map/dot_general | solution.py:64
  483.4 3.8 psum.7
  487.2 19.5 %multiply_convert_fusion = (bf16[1024,4096]{1,0:T(8,128)(2,1)}, bf16[1024,4096]{1,0:T(8,128)(2,1)}) fusion(f32[1024,4096]{1,0:T(8,128)} %get-tuple-element.73, f32[4096]{0:T(1024)S(1)} %copy-done.1, f32[1024]{0:T(1024)S(1)} %add_rsqrt_fusion), kind=kLoop, calls=%fused_computation.30 | loop fusion | flops 16777216 | bytes 33574912 | tf_op jit(solution)/shard_map/convert_element_type | solution.py:73
  (10 shorter events, 0.2 us)
Async XLA Ops:
  9.0 11.8 %all-to-all-start.1 = ((bf16[512,2,256]{2,0,1:T(8,128)(2,1)}), bf16[512,2,256]{2,0,1:T(8,128)(2,1)S(1)}, u32[]{:S(2)}, u32[]{:S(2)}) async-start(bf16[512,2,256]{2,0,1:T(8,128)(2,1)} %bitcast.59), calls=%async_computation.1 | async-start | bytes 1048576 | tf_op jit(solution)/shard_map/all_to_all | solution.py:59
  20.8 10.3 %all-to-all-start.2 = ((bf16[512,2,256]{2,0,1:T(8,128)(2,1)}), bf16[512,2,256]{2,0,1:T(8,128)(2,1)S(1)}, u32[]{:S(2)}, u32[]{:S(2)}) async-start(bf16[512,2,256]{2,0,1:T(8,128)(2,1)} %bitcast.58), calls=%async_computation.2 | async-start | bytes 1048576 | tf_op jit(solution)/shard_map/all_to_all | solution.py:60
  31.1 50.9 %all-to-all-start = ((bf16[512,2,2048]{2,0,1:T(8,128)(2,1)}), bf16[512,2,2048]{2,0,1:T(8,128)(2,1)}, u32[]{:S(2)}, u32[]{:S(2)}) async-start(bf16[512,2,2048]{2,0,1:T(8,128)(2,1)} %bitcast.71), calls=%async_computation | async-start | bytes 8388608 | tf_op jit(solution)/shard_map/all_to_all | solution.py:58
  36.7 50.9 %copy-start = (s32[1,1024]{1,0:T(1,128)S(1)}, s32[1,1024]{1,0:T(1,128)}, u32[]{:S(2)}) copy-start(s32[1,1024]{1,0:T(1,128)} %param.12) | copy-start | bytes 12292
  36.7 231.5 %all-gather.3.cloned.1.call-start = ((), (), s32[]{:S(2)}) async-start(), calls=%async_computation.3 | async-start | bytes 12582912 | tf_op jit(solution)/shard_map/all_gather | solution.py:63
  161.7 276.6 %all-gather.5.cloned.1.call-start = ((), (), s32[]{:S(2)}) async-start(), calls=%async_computation.4 | async-start | bytes 35651584 | tf_op jit(solution)/shard_map/all_gather | solution.py:66
  162.5 324.7 %copy-start.1 = (f32[4096]{0:T(1024)S(1)}, f32[4096]{0:T(1024)}, u32[]{:S(2)}) copy-start(f32[4096]{0:T(1024)} %param.15) | copy-start | bytes 49156
Sparse Core Ops, SparseCore 0:
  161.8 106.3 all-gather.2
  269.8 168.4 all-gather.4
where the time goes:
time: 516 us; the launch traced here: 514 us
  waiting for transfers between devices  328 us (64%)
  matrix products  106 us (21%)
  local copies, waits for them, and re-layouts  28.5 us (6%)
  other arithmetic  20.7 us (4%)
  between operations  14.1 us (3%)
  starting transfers between devices  12.7 us (2%)
    all_gather x1, waiting for transfers between devices, body(): lax.all_gather(out_weight, 'col', axis=0, tiled=True)  170 us
    all_gather x1, waiting for transfers between devices, body(): panel_rows = lax.all_gather(attn, 'row', axis=1, tiled=True)  106 us
    dot_general x1, matrix products, body(): jnp.dot(panel_rows, lax.all_gather(out_weight, 'col', axis=0, tiled=True)...  45.1 us
    all_to_all x1, waiting for transfers between devices, body(): lax.all_to_all(query_proj, 'row', split_axis=1, concat_axis=0, tiled=True)  43.2 us
    sub x2, matrix products, one_group(): weights = jnp.where(allowed, jnp.exp(scores - peak), jnp.float32(0.0))  40.3 us
    dot_general x2, matrix products, one_group(): jnp.einsum('gqk,kd->gqd', probs, group_value, preferred_element_type=jnp....  20.2 us
    convert_element_type x1, other arithmetic, body(): return (hidden_sum.astype(jnp.bfloat16), normed.astype(jnp.bfloat16))  19.5 us
  transfers between devices with their start and end apart: 5, of which 5 were waited for; matrix products, arithmetic and copies ran while one was open for 2% of the time, Pallas kernels for 0%

commit v1 on v0

--- a/solution.py
+++ b/solution.py
@@ -1,11 +1,17 @@
+import functools
+import math
+
 import jax
 import jax.numpy as jnp
 from jax import lax
+from jax.experimental import pallas as pl
+from jax.experimental.pallas import tpu as pltpu
 from jax.sharding import PartitionSpec as P
 
 D = 8192
 HD = 128
 HK = 4
+MESH = pl.DeviceIdType.MESH
 
 
 def attend_local(query_heads, key_heads, value_heads, segment_row):
@@ -49,7 +55,7 @@
     return spread.reshape(rows_local, kv_count * repeat * HD)
 
 
-def body(query_proj, key_proj, value_proj, segment_ids, out_weight, residual, norm_gain):
+def body_any(query_proj, key_proj, value_proj, segment_ids, out_weight, residual, norm_gain):
     row_count = lax.axis_size("row")
     repeat = max(row_count // HK, 1)
     key_wide = widen_heads(key_proj, repeat)
@@ -73,6 +79,377 @@
     return (hidden_sum.astype(jnp.bfloat16), normed.astype(jnp.bfloat16))
 
 
+NZ = 4
+CH = 4
+QT = 256
+KT = 768
+STEPS = 8
+NB = 512
+
+
+def fused_kernel(q_ref, k_ref, v_ref, seg_row, seg_col, w_ref, res_ref,
+                 hid_ref, sq_ref, wfull,
+                 qbuf, kbuf, vbuf, bias, attn, wbuf, obuf, acc, sqbuf,
+                 send, recv, loc, lw, a_send, a_recv, x_send, x_recv, osem):
+    r = lax.axis_index("row")
+    col = lax.axis_index("col")
+    core = lax.rem(col, 2)
+    y = lax.rem(col // 2, 2)
+    z = col // 4
+    half = q_ref.shape[0]
+    wrows = w_ref.shape[0]
+    crow = wrows // CH
+    width = w_ref.shape[1]
+
+    def cid(zz, yy, cc):
+        return (zz * 2 + yy) * 2 + cc
+
+    right = (r, cid(z + 1, y, core))
+    left = (r, cid(z - 1, y, core))
+    across = (r, cid(z, 1 - y, core))
+    sibling = (r, cid(z, y, 1 - core))
+    partner = (1 - r, col)
+
+    barrier = pltpu.get_barrier_semaphore()
+
+    def greet(dev):
+        pl.semaphore_signal(barrier, inc=1, device_id=dev, device_id_type=MESH)
+
+    greet(across)
+    greet(sibling)
+    greet(partner)
+
+    @pl.when(z > 0)
+    def _():
+        greet(left)
+
+    @pl.when(z < NZ - 1)
+    def _():
+        greet(right)
+
+    at_end = (z == 0) | (z == NZ - 1)
+
+    @pl.when(at_end)
+    def _():
+        pl.semaphore_wait(barrier, 4)
+
+    @pl.when(jnp.logical_not(at_end))
+    def _():
+        pl.semaphore_wait(barrier, 5)
+
+    def wcopy(way, dev, zz, yy, j, own):
+        slot = cid(zz, yy, core)
+        rows = pl.ds(j * crow, crow)
+        src = w_ref.at[rows, :] if own else wfull.at[slot, rows, :]
+        return pltpu.make_async_remote_copy(
+            src_ref=src, dst_ref=wfull.at[slot, rows, :],
+            send_sem=send.at[way, zz * 2 + yy, j], recv_sem=recv.at[slot, j],
+            device_id=dev, device_id_type=MESH)
+
+    def wait_chunk(slot, j):
+        rows = pl.ds(j * crow, crow)
+        pltpu.make_async_copy(wfull.at[slot, rows, :], wfull.at[slot, rows, :], recv.at[slot, j]).wait()
+
+    own_w = pltpu.make_async_copy(w_ref, wfull.at[col], loc.at[0])
+    k_local = pltpu.make_async_copy(k_ref, kbuf.at[pl.ds(r * half, half), :], loc.at[1])
+    v_local = pltpu.make_async_copy(v_ref, vbuf.at[pl.ds(r * half, half), :], loc.at[2])
+    q_local = pltpu.make_async_copy(q_ref, qbuf, loc.at[3])
+    res_local = pltpu.make_async_copy(res_ref, obuf, loc.at[4])
+
+    def kv_remote(src, dst, i):
+        return pltpu.make_async_remote_copy(
+            src_ref=src, dst_ref=dst.at[pl.ds(r * half, half), :],
+            send_sem=x_send.at[i], recv_sem=x_recv.at[i],
+            device_id=partner, device_id_type=MESH)
+
+    k_rem = kv_remote(k_ref, kbuf, 0)
+    v_rem = kv_remote(v_ref, vbuf, 1)
+    k_rem.start()
+    v_rem.start()
+    for j in range(CH):
+        @pl.when(z < NZ - 1)
+        def _():
+            wcopy(0, right, z, y, j, True).start()
+
+        @pl.when(z > 0)
+        def _():
+            wcopy(1, left, z, y, j, True).start()
+
+        wcopy(2, across, z, y, j, True).start()
+    k_local.start()
+    v_local.start()
+    q_local.start()
+    res_local.start()
+    own_w.start()
+    for j in range(CH):
+        wcopy(3, sibling, z, y, j, True).start()
+
+    scale = HD ** (-0.5) * math.log2(math.e)
+    starts = []
+    for i in range(half // QT):
+        t0 = pl.multiple_of(r * half + i * QT, QT)
+        ks = pl.multiple_of(jnp.maximum(t0 + QT - KT, 0), QT)
+        starts.append((t0, ks))
+        qs = seg_col[pl.ds(t0, QT), :]
+        ksg = seg_row[:, pl.ds(ks, KT)]
+        qp = t0 + lax.broadcasted_iota(jnp.int32, (QT, KT), 0)
+        kp = ks + lax.broadcasted_iota(jnp.int32, (QT, KT), 1)
+        keep = (qs == ksg) & (kp <= qp)
+        bias[i] = jnp.where(keep, jnp.float32(0.0), jnp.float32(-1e30))
+
+    q_local.wait()
+    k_local.wait()
+    v_local.wait()
+    k_rem.wait_recv()
+    v_rem.wait_recv()
+
+    heads = qbuf.shape[1] // HD
+    per_step = heads // STEPS
+    aw = per_step * HD
+    group = heads // HK
+
+    def attn_copy(g):
+        cols = pl.ds(pl.multiple_of(g * aw, aw), aw)
+        part = attn.at[pl.ds(pl.multiple_of(r * half, half), half), cols]
+        return pltpu.make_async_remote_copy(
+            src_ref=part, dst_ref=part, send_sem=a_send.at[g], recv_sem=a_recv.at[g],
+            device_id=partner, device_id_type=MESH)
+
+    @pl.loop(0, STEPS)
+    def _(g):
+        kcol = pl.ds(pl.multiple_of((g * per_step // group) * HD, HD), HD)
+        for i, (t0, ks) in enumerate(starts):
+            key = kbuf[pl.ds(ks, KT), kcol]
+            val = vbuf[pl.ds(ks, KT), kcol]
+            for h in range(per_step):
+                hc = pl.ds(pl.multiple_of(g * aw + h * HD, HD), HD)
+                qh = qbuf[i * QT:(i + 1) * QT, hc]
+                s = lax.dot_general(qh, key, (((1,), (1,)), ((), ())),
+                                    preferred_element_type=jnp.float32)
+                s = s * scale + bias[i]
+                m = jnp.max(s, axis=1, keepdims=True)
+                p = jnp.exp2(s - m)
+                tot = jnp.sum(p, axis=1, keepdims=True)
+                o = jnp.dot(p.astype(jnp.bfloat16), val, preferred_element_type=jnp.float32)
+                attn[pl.ds(t0, QT), hc] = (o / tot).astype(jnp.bfloat16)
+        attn_copy(g).start()
+
+    def place(t):
+        h = (t + 1) // 2
+        return z - h if t % 2 == 1 else z + h
+
+    def guard(t, f):
+        if t == 0:
+            f()
+        elif t % 2 == 1:
+            pl.when(place(t) >= 0)(f)
+        else:
+            pl.when(place(t) < NZ)(f)
+
+    def forward(t):
+        def go():
+            zz = place(t)
+
+            @pl.loop(0, CH)
+            def _(j):
+                wait_chunk(cid(zz, y, core), j)
+                if t % 2 == 1:
+                    @pl.when(z < NZ - 1)
+                    def _():
+                        wcopy(0, right, zz, y, j, False).start()
+                else:
+                    @pl.when(z > 0)
+                    def _():
+                        wcopy(1, left, zz, y, j, False).start()
+                wcopy(2, across, zz, y, j, False).start()
+                wcopy(3, sibling, zz, y, j, False).start()
+        guard(t, go)
+
+    def forward_y(t):
+        def go():
+            zz = place(t)
+
+            @pl.loop(0, CH)
+            def _(j):
+                wait_chunk(cid(zz, 1 - y, core), j)
+                wcopy(3, sibling, zz, 1 - y, j, False).start()
+        guard(t, go)
+
+    nsteps = width // NB
+
+    def project(t, yy):
+        def go():
+            zz = place(t)
+
+            @pl.loop(0, CH)
+            def _(j):
+                wait_chunk(cid(zz, yy, 1 - core), j)
+
+            first = cid(zz, yy, 0)
+
+            def wload(n, c):
+                cols = pl.ds(pl.multiple_of(n * NB, NB), NB)
+                return pltpu.make_async_copy(
+                    wfull.at[first + c, :, cols], wbuf.at[pl.ds(c * wrows, wrows), cols],
+                    lw.at[c, n])
+
+            @pl.loop(0, nsteps)
+            def _(n):
+                wload(n, 0).start()
+                wload(n, 1).start()
+
+            kc = pl.ds(pl.multiple_of(first * wrows, 2 * wrows), 2 * wrows)
+
+            @pl.loop(0, nsteps)
+            def _(n):
+                cols = pl.ds(pl.multiple_of(n * NB, NB), NB)
+                wload(n, 0).wait()
+                wload(n, 1).wait()
+                acc[:, cols] += jnp.dot(attn[:, kc], wbuf[:, cols],
+                                        preferred_element_type=jnp.float32)
+        guard(t, go)
+
+    forward(1)
+    forward(2)
+    res_local.wait()
+
+    @pl.loop(0, nsteps)
+    def _(n):
+        cols = pl.ds(pl.multiple_of(n * NB, NB), NB)
+        acc[:, cols] = obuf[:, cols].astype(jnp.float32)
+
+    own_w.wait()
+    forward_y(0)
+    forward(3)
+    forward(4)
+
+    @pl.loop(0, STEPS)
+    def _(g):
+        attn_copy(g).wait_send()
+        cols = pl.ds(pl.multiple_of(g * aw, aw), aw)
+        part = attn.at[pl.ds(pl.multiple_of((1 - r) * half, half), half), cols]
+        pltpu.make_async_copy(part, part, a_recv.at[g]).wait()
+
+    project(0, y)
+    project(1, y)
+    project(2, y)
+    forward(5)
+    forward(6)
+    project(0, 1 - y)
+    forward_y(1)
+    forward_y(2)
+    project(3, y)
+    project(4, y)
+    project(1, 1 - y)
+    project(2, 1 - y)
+    forward_y(3)
+    forward_y(4)
+    project(5, y)
+    project(6, y)
+    project(3, 1 - y)
+    project(4, 1 - y)
+    forward_y(5)
+    forward_y(6)
+    project(5, 1 - y)
+    project(6, 1 - y)
+
+    def out_copy(n):
+        cols = pl.ds(pl.multiple_of(n * NB, NB), NB)
+        return pltpu.make_async_copy(obuf.at[:, cols], hid_ref.at[:, cols], osem.at[n])
+
+    def finish(n, part):
+        cols = pl.ds(pl.multiple_of(n * NB, NB), NB)
+        a = acc[:, cols]
+        obuf[:, cols] = a.astype(jnp.bfloat16)
+        out_copy(n).start()
+        sqr = a * a
+        for i in range(NB // 128):
+            part = part + sqr[:, i * 128:(i + 1) * 128]
+        return part
+
+    part = lax.fori_loop(0, nsteps, finish, jnp.zeros((acc.shape[0], 128), jnp.float32))
+    sqbuf[0] = jnp.sum(part.T, axis=0, keepdims=True)
+    x_sq = pltpu.make_async_remote_copy(
+        src_ref=sqbuf.at[0], dst_ref=sqbuf.at[1], send_sem=x_send.at[2], recv_sem=x_recv.at[2],
+        device_id=partner, device_id_type=MESH)
+    x_sq.start()
+
+    k_rem.wait_send()
+    v_rem.wait_send()
+    for t in range(2 * NZ - 1):
+        def sent(t=t):
+            zz = place(t)
+
+            @pl.loop(0, CH)
+            def _(j):
+                if t % 2 == 1 or t == 0:
+                    @pl.when(z < NZ - 1)
+                    def _():
+                        wcopy(0, right, zz, y, j, False).wait_send()
+                if t % 2 == 0:
+                    @pl.when(z > 0)
+                    def _():
+                        wcopy(1, left, zz, y, j, False).wait_send()
+                wcopy(2, across, zz, y, j, False).wait_send()
+                wcopy(3, sibling, zz, y, j, False).wait_send()
+                wcopy(3, sibling, zz, 1 - y, j, False).wait_send()
+        guard(t, sent)
+
+    @pl.loop(0, nsteps)
+    def _(n):
+        out_copy(n).wait()
+
+    x_sq.wait()
+    sq_ref[...] = sqbuf[0] + sqbuf[1]
+
+
+def body_fused(query_proj, key_proj, value_proj, segment_ids, out_weight, residual, norm_gain):
+    half, qw = query_proj.shape
+    length = segment_ids.shape[1]
+    wrows, width = out_weight.shape
+    cols = lax.axis_size("col")
+    hbm = pl.BlockSpec(memory_space=pl.ANY)
+    vmem = pl.BlockSpec(memory_space=pltpu.VMEM)
+    dma = pltpu.SemaphoreType.DMA
+    hidden, squares, _ = pl.pallas_call(
+        fused_kernel,
+        out_shape=(
+            jax.ShapeDtypeStruct((length, width), jnp.bfloat16),
+            jax.ShapeDtypeStruct((1, length), jnp.float32),
+            jax.ShapeDtypeStruct((cols, wrows, width), jnp.bfloat16),
+        ),
+        in_specs=[hbm, hbm, hbm, vmem, vmem, hbm, hbm],
+        out_specs=(hbm, vmem, hbm),
+        scratch_shapes=[
+            pltpu.VMEM((half, qw), jnp.bfloat16),
+            pltpu.VMEM((length, HK * HD), jnp.bfloat16),
+            pltpu.VMEM((length, HK * HD), jnp.bfloat16),
+            pltpu.VMEM((half // QT, QT, KT), jnp.float32),
+            pltpu.VMEM((length, qw), jnp.bfloat16),
+            pltpu.VMEM((2 * wrows, width), jnp.bfloat16),
+            pltpu.VMEM((length, width), jnp.bfloat16),
+            pltpu.VMEM((length, width), jnp.float32),
+            pltpu.VMEM((2, 1, length), jnp.float32),
+            dma((4, cols // 2, CH)),
+            dma((cols, CH)),
+            dma((5,)),
+            dma((2, width // NB)),
+            dma((STEPS,)),
+            dma((STEPS,)),
+            dma((3,)),
+            dma((3,)),
+            dma((width // NB,)),
+        ],
+        compiler_params=pltpu.CompilerParams(
+            collective_id=0, has_side_effects=True, vmem_limit_bytes=60 * 1024 * 1024),
+        name="fused",
+    )(query_proj, key_proj, value_proj, segment_ids, segment_ids.reshape(length, 1),
+      out_weight, residual)
+    scaled = lax.rsqrt(squares[0] / D + jnp.float32(1e-05))
+    normed = hidden.astype(jnp.float32) * scaled[:, None] * norm_gain[None, :]
+    return hidden, normed.astype(jnp.bfloat16)
+
+
 def solution(mesh):
     placed = (
         P(("col", "row"), None),
@@ -83,8 +460,9 @@
         P("col", "row"),
         P("row"),
     )
+    known = mesh.shape["row"] == 2 and mesh.shape["col"] == 4 * NZ
     return jax.shard_map(
-        body,
+        body_fused if known else body_any,
         mesh=mesh,
         in_specs=placed,
         out_specs=(P("col", "row"), P("col", "row")),

time: 516 us -> 229 us (0.44)
  waiting for transfers between devices: 328 us -> 0 us
  Pallas kernels: 0 us -> 207 us
  matrix products: 106 us -> 0 us
  local copies, waits for them, and re-layouts: 28.5 us -> 9.6 us
  between operations: 14.1 us -> 0.66 us
  starting transfers between devices: 12.7 us -> 0 us
  other arithmetic: 20.7 us -> 11.2 us
    all_gather x2 -> x0, waiting for transfers between devices: 276 us -> none  [the longest x1 170 us: body(): lax.all_gather(out_weight, 'col', axis=0, tiled=True)]
    pallas_call x0 -> x1, Pallas kernels: none -> 207 us  [body_fused(): pl.pallas_call(fused_kernel, out_shape=(jax.ShapeDtypeStruct((length, wid...]
    dot_general x3 -> x0, matrix products: 65.3 us -> none  [the longest x1 45.1 us: body(): jnp.dot(panel_rows, lax.all_gather(out_weight, 'col', axis=0, tiled=True)...]
    all_to_all x3 -> x0, waiting for transfers between devices: 51.6 us -> none  [the longest x1 43.2 us: body(): lax.all_to_all(query_proj, 'row', split_axis=1, concat_axis=0, tiled=True)]
    sub x2 -> x0, matrix products: 40.3 us -> none  [one_group(): weights = jnp.where(allowed, jnp.exp(scores - peak), jnp.float32(0.0))]
    all_to_all x3 -> x0, starting transfers between devices: 12.6 us -> none  [the longest x1 5.62 us: body(): lax.all_to_all(query_proj, 'row', split_axis=1, concat_axis=0, tiled=True)]
    convert_element_type x1, other arithmetic: 19.5 us -> 10.5 us  [body_fused(): return (hidden, normed.astype(jnp.bfloat16))]
    dynamic_update_slice x4 -> x0, local copies, waits for them, and re-layouts: 8.93 us -> none  [attend_local(): heads_out = lax.map(one_group, (query_grid, key_grid, value_grid))]
  transfers between devices with their start and end apart: 5 -> 0, of which waited for: 5 -> 0; matrix products, arithmetic and copies ran while one was open for 2% -> 0% of each run, Pallas kernels for 0% -> 0%
where the time goes in v1:
time: 229 us
  Pallas kernels  207 us (90%)
  other arithmetic  11.2 us (5%)
  local copies, waits for them, and re-layouts  9.6 us (4%)
    pallas_call x1, Pallas kernels, body_fused(): pl.pallas_call(fused_kernel, out_shape=(jax.ShapeDtypeStruct((length, wid...  207 us
    convert_element_type x1, other arithmetic, body_fused(): return (hidden, normed.astype(jnp.bfloat16))  10.5 us
    unnamed x3, local copies, waits for them, and re-layouts  7.89 us

profile of v1, /device:TPU:1, one launch (start us, length us, event | category | flops | bytes accessed | tf_op | source)
XLA Modules:
  0.0 228.9 jit_solution(15160713822983165344)
XLA Ops:
  0.6 0.0 copy-start
  0.6 1.7 copy.9.seg_col
  2.4 207.5 %fused.1 = (bf16[1024,4096]{1,0:T(8,128)(2,1)}, f32[1,1024]{1,0:T(1,128)}, bf16[16,256,4096]{2,1,0:T(8,128)(2,1)}) custom-call(bf16[512,4096]{1,0:T(8,128)(2,1)} %q_ref.1, bf16[512,512]{1,0:T(8,128)(2,1)} %k_ref.1, bf16[512,512]{1,0:T(8,128)(2,1)} %v_ref.1, s32[1,1024]{1,0:T(1,128)} %seg_row.1, s32[1024,1]{1,0:T(8,128)} %copy.9.seg_col, ...), custom_call_target="tpu_custom_call" | custom-call | tf_op jit(solution)/shard_map/fused/pallas_call | solution.py:414
  209.8 0.7 add_rsqrt_fusion
  210.5 0.0 copy-done
  210.5 10.5 %multiply_convert_fusion = bf16[1024,4096]{1,0:T(8,128)(2,1)} fusion(bf16[1024,4096]{1,0:T(8,128)(2,1)} %get-tuple-element.8, f32[4096]{0:T(1024)S(1)} %copy-done, f32[1024]{0:T(1024)S(1)} %bitcast.3), kind=kLoop, calls=%fused_computation | loop fusion | flops 16777216 | bytes 16797696 | tf_op jit(solution)/shard_map/convert_element_type | solution.py:450
  221.0 7.9 %copy.11 = bf16[1024,4096]{1,0:T(8,128)(2,1)} copy(bf16[1024,4096]{1,0:T(8,128)(2,1)} %get-tuple-element.8) | data formatting | bytes 16777216
Async XLA Ops:
  0.6 209.9 %copy-start = (f32[4096]{0:T(1024)S(1)}, f32[4096]{0:T(1024)}, u32[]{:S(2)}) copy-start(f32[4096]{0:T(1024)} %param.13) | copy-start | bytes 49156

commit v2 on v1

--- a/solution.py
+++ b/solution.py
@@ -80,14 +80,14 @@
 
 
 NZ = 4
-CH = 4
+CH = 8
 QT = 256
 KT = 768
 STEPS = 8
 NB = 512
 
 
-def fused_kernel(q_ref, k_ref, v_ref, seg_row, seg_col, w_ref, res_ref,
+def fused_kernel(q_ref, k_ref, v_ref, seg_row, w_ref, res_ref,
                  hid_ref, sq_ref, wfull,
                  qbuf, kbuf, vbuf, bias, attn, wbuf, obuf, acc, sqbuf,
                  send, recv, loc, lw, a_send, a_recv, x_send, x_recv, osem):
@@ -166,6 +166,7 @@
     v_rem = kv_remote(v_ref, vbuf, 1)
     k_rem.start()
     v_rem.start()
+    wcopy(2, across, z, y, CH - 1, True).start()
     for j in range(CH):
         @pl.when(z < NZ - 1)
         def _():
@@ -175,7 +176,8 @@
         def _():
             wcopy(1, left, z, y, j, True).start()
 
-        wcopy(2, across, z, y, j, True).start()
+        if j < CH - 1:
+            wcopy(2, across, z, y, j, True).start()
     k_local.start()
     v_local.start()
     q_local.start()
@@ -184,14 +186,85 @@
     for j in range(CH):
         wcopy(3, sibling, z, y, j, True).start()
 
+    def place(t):
+        h = (t + 1) // 2
+        return z - h if t % 2 == 1 else z + h
+
+    def guard(t, f):
+        if t == 0:
+            f()
+        elif t % 2 == 1:
+            pl.when(place(t) >= 0)(f)
+        else:
+            pl.when(place(t) < NZ)(f)
+
+    def on_z(t, yy, j, act):
+        zz = place(t)
+        if t % 2 == 1 or t == 0:
+            @pl.when(z < NZ - 1)
+            def _():
+                act(wcopy(0, right, zz, yy, j, False))
+        if t % 2 == 0:
+            @pl.when(z > 0)
+            def _():
+                act(wcopy(1, left, zz, yy, j, False))
+
+    def begin(c):
+        c.start()
+
+    def forward_chunk(t, j):
+        def go():
+            zz = place(t)
+            wait_chunk(cid(zz, y, core), j)
+            on_z(t, y, j, begin)
+
+            @pl.when(j < CH - 1)
+            def _():
+                wcopy(2, across, zz, y, j, False).start()
+
+            wcopy(3, sibling, zz, y, j, False).start()
+        guard(t, go)
+
+    def forward(t):
+        @pl.loop(0, CH)
+        def _(j):
+            forward_chunk(t, j)
+
+    def forward_last(t):
+        def go():
+            zz = place(t)
+            wait_chunk(cid(zz, 1 - y, core), CH - 1)
+            on_z(t, 1 - y, CH - 1, begin)
+            wcopy(3, sibling, zz, 1 - y, CH - 1, False).start()
+        guard(t, go)
+
+    def forward_y(t):
+        def go():
+            zz = place(t)
+
+            @pl.loop(0, CH - 1)
+            def _(j):
+                wait_chunk(cid(zz, 1 - y, core), j)
+                wcopy(3, sibling, zz, 1 - y, j, False).start()
+        guard(t, go)
+
+    nsteps = width // NB
+    res_local.wait()
+
+    @pl.loop(0, nsteps)
+    def _(n):
+        cols = pl.ds(pl.multiple_of(n * NB, NB), NB)
+        acc[:, cols] = obuf[:, cols].astype(jnp.float32)
+
     scale = HD ** (-0.5) * math.log2(math.e)
     starts = []
     for i in range(half // QT):
         t0 = pl.multiple_of(r * half + i * QT, QT)
         ks = pl.multiple_of(jnp.maximum(t0 + QT - KT, 0), QT)
         starts.append((t0, ks))
-        qs = seg_col[pl.ds(t0, QT), :]
-        ksg = seg_row[:, pl.ds(ks, KT)]
+        qrow = seg_row[:, pl.ds(t0, QT)].astype(jnp.float32)
+        qs = jnp.broadcast_to(qrow, (128, QT)).T[:, :1]
+        ksg = seg_row[:, pl.ds(ks, KT)].astype(jnp.float32)
         qp = t0 + lax.broadcasted_iota(jnp.int32, (QT, KT), 0)
         kp = ks + lax.broadcasted_iota(jnp.int32, (QT, KT), 1)
         keep = (qs == ksg) & (kp <= qp)
@@ -233,49 +306,9 @@
                 o = jnp.dot(p.astype(jnp.bfloat16), val, preferred_element_type=jnp.float32)
                 attn[pl.ds(t0, QT), hc] = (o / tot).astype(jnp.bfloat16)
         attn_copy(g).start()
-
-    def place(t):
-        h = (t + 1) // 2
-        return z - h if t % 2 == 1 else z + h
-
-    def guard(t, f):
-        if t == 0:
-            f()
-        elif t % 2 == 1:
-            pl.when(place(t) >= 0)(f)
-        else:
-            pl.when(place(t) < NZ)(f)
-
-    def forward(t):
-        def go():
-            zz = place(t)
-
-            @pl.loop(0, CH)
-            def _(j):
-                wait_chunk(cid(zz, y, core), j)
-                if t % 2 == 1:
-                    @pl.when(z < NZ - 1)
-                    def _():
-                        wcopy(0, right, zz, y, j, False).start()
-                else:
-                    @pl.when(z > 0)
-                    def _():
-                        wcopy(1, left, zz, y, j, False).start()
-                wcopy(2, across, zz, y, j, False).start()
-                wcopy(3, sibling, zz, y, j, False).start()
-        guard(t, go)
-
-    def forward_y(t):
-        def go():
-            zz = place(t)
-
-            @pl.loop(0, CH)
-            def _(j):
-                wait_chunk(cid(zz, 1 - y, core), j)
-                wcopy(3, sibling, zz, 1 - y, j, False).start()
-        guard(t, go)
-
-    nsteps = width // NB
+        for t in (1, 2):
+            forward_chunk(t, g)
+
 
     def project(t, yy):
         def go():
@@ -309,19 +342,15 @@
                                         preferred_element_type=jnp.float32)
         guard(t, go)
 
-    forward(1)
-    forward(2)
-    res_local.wait()
-
-    @pl.loop(0, nsteps)
-    def _(n):
-        cols = pl.ds(pl.multiple_of(n * NB, NB), NB)
-        acc[:, cols] = obuf[:, cols].astype(jnp.float32)
-
+    forward_last(0)
     own_w.wait()
     forward_y(0)
+    forward_last(1)
+    forward_last(2)
     forward(3)
     forward(4)
+    forward_last(3)
+    forward_last(4)
 
     @pl.loop(0, STEPS)
     def _(g):
@@ -335,6 +364,8 @@
     project(2, y)
     forward(5)
     forward(6)
+    forward_last(5)
+    forward_last(6)
     project(0, 1 - y)
     forward_y(1)
     forward_y(2)
@@ -380,19 +411,20 @@
         def sent(t=t):
             zz = place(t)
 
+            def ended(c):
+                c.wait_send()
+
             @pl.loop(0, CH)
             def _(j):
-                if t % 2 == 1 or t == 0:
-                    @pl.when(z < NZ - 1)
-                    def _():
-                        wcopy(0, right, zz, y, j, False).wait_send()
-                if t % 2 == 0:
-                    @pl.when(z > 0)
-                    def _():
-                        wcopy(1, left, zz, y, j, False).wait_send()
-                wcopy(2, across, zz, y, j, False).wait_send()
+                on_z(t, y, j, ended)
                 wcopy(3, sibling, zz, y, j, False).wait_send()
                 wcopy(3, sibling, zz, 1 - y, j, False).wait_send()
+
+            @pl.loop(0, CH - 1 if t else CH)
+            def _(j):
+                wcopy(2, across, zz, y, j, False).wait_send()
+
+            on_z(t, 1 - y, CH - 1, ended)
         guard(t, sent)
 
     @pl.loop(0, nsteps)
@@ -401,6 +433,17 @@
 
     x_sq.wait()
     sq_ref[...] = sqbuf[0] + sqbuf[1]
+
+
+def norm_kernel(hid_ref, sq_ref, gain_ref, sum_ref, out_ref):
+    rows, width = hid_ref.shape
+    scaled = lax.rsqrt(sq_ref[...] / D + jnp.float32(1e-05))
+    column = jnp.broadcast_to(scaled, (128, rows)).T[:, :1]
+    for n in range(width // NB):
+        cols = slice(n * NB, (n + 1) * NB)
+        hid = hid_ref[:, cols]
+        sum_ref[:, cols] = hid
+        out_ref[:, cols] = (hid.astype(jnp.float32) * column * gain_ref[:, cols]).astype(jnp.bfloat16)
 
 
 def body_fused(query_proj, key_proj, value_proj, segment_ids, out_weight, residual, norm_gain):
@@ -418,7 +461,7 @@
             jax.ShapeDtypeStruct((1, length), jnp.float32),
             jax.ShapeDtypeStruct((cols, wrows, width), jnp.bfloat16),
         ),
-        in_specs=[hbm, hbm, hbm, vmem, vmem, hbm, hbm],
+        in_specs=[hbm, hbm, hbm, vmem, hbm, hbm],
         out_specs=(hbm, vmem, hbm),
         scratch_shapes=[
             pltpu.VMEM((half, qw), jnp.bfloat16),
@@ -443,11 +486,20 @@
         compiler_params=pltpu.CompilerParams(
             collective_id=0, has_side_effects=True, vmem_limit_bytes=60 * 1024 * 1024),
         name="fused",
-    )(query_proj, key_proj, value_proj, segment_ids, segment_ids.reshape(length, 1),
+    )(query_proj, key_proj, value_proj, segment_ids,
       out_weight, residual)
-    scaled = lax.rsqrt(squares[0] / D + jnp.float32(1e-05))
-    normed = hidden.astype(jnp.float32) * scaled[:, None] * norm_gain[None, :]
-    return hidden, normed.astype(jnp.bfloat16)
+    rows = 128
+    tile = pl.BlockSpec((rows, width), lambda i: (i, 0))
+    return tuple(pl.pallas_call(
+        norm_kernel,
+        grid=(length // rows,),
+        out_shape=(jax.ShapeDtypeStruct((length, width), jnp.bfloat16),) * 2,
+        in_specs=[tile, pl.BlockSpec((1, rows), lambda i: (0, i)),
+                  pl.BlockSpec((1, width), lambda i: (0, 0))],
+        out_specs=(tile, tile),
+        compiler_params=pltpu.CompilerParams(vmem_limit_bytes=32 * 1024 * 1024),
+        name="norm",
+    )(hidden, squares, norm_gain.reshape(1, width)))
 
 
 def solution(mesh):

time: 229 us -> 225 us (0.983)
  Pallas kernels: 207 us -> 220 us
  other arithmetic: 11.2 us -> 0 us
  local copies, waits for them, and re-layouts: 9.6 us -> 4.05 us
    convert_element_type x1 -> x0, other arithmetic: 10.5 us -> none  [body_fused(): return (hidden, normed.astype(jnp.bfloat16))]
    pallas_call x0 -> x1, Pallas kernels: none -> 7.1 us  [body_fused(): pl.pallas_call(norm_kernel, grid=(length // rows,), out_shape=(jax.ShapeD...]
    pallas_call x1, Pallas kernels: 207 us -> 213 us  [body_fused(): pl.pallas_call(fused_kernel, out_shape=(jax.ShapeDtypeStruct((length, wid...]
    unnamed x3 -> x6, local copies, waits for them, and re-layouts: 7.89 us -> 4.05 us
where the time goes in v2:
time: 225 us
  Pallas kernels  220 us (98%)
  local copies, waits for them, and re-layouts  4.05 us (2%)
    pallas_call x1, Pallas kernels, body_fused(): pl.pallas_call(fused_kernel, out_shape=(jax.ShapeDtypeStruct((length, wid...  213 us
    pallas_call x1, Pallas kernels, body_fused(): pl.pallas_call(norm_kernel, grid=(length // rows,), out_shape=(jax.ShapeD...  7.1 us

profile of v2, /device:TPU:1, one launch (start us, length us, event | category | flops | bytes accessed | tf_op | source)
XLA Modules:
  0.0 224.9 jit_solution(18174605965895215926)
XLA Ops:
  0.6 0.0 copy-start.1
  0.6 213.1 %fused.1 = (bf16[1024,4096]{1,0:T(8,128)(2,1)}, f32[1,1024]{1,0:T(1,128)}, bf16[16,256,4096]{2,1,0:T(8,128)(2,1)}) custom-call(bf16[512,4096]{1,0:T(8,128)(2,1)} %q_ref.1, bf16[512,512]{1,0:T(8,128)(2,1)} %k_ref.1, bf16[512,512]{1,0:T(8,128)(2,1)} %v_ref.1, s32[1,1024]{1,0:T(1,128)} %seg_row.1, bf16[256,4096]{1,0:T(8,128)(2,1)} %w_ref.1, ...), custom_call_target="tpu_custom_call" | custom-call | tf_op jit(solution)/shard_map/fused/pallas_call | solution.py:457
  213.8 0.0 copy-done.1
  213.8 0.0 copy-start
  213.8 3.4 %copy-done = bf16[1024,4096]{1,0:T(8,128)(2,1)S(1)} copy-done((bf16[1024,4096]{1,0:T(8,128)(2,1)S(1)}, bf16[1024,4096]{1,0:T(8,128)(2,1)}, u32[]{:S(2)}) %copy-start) | copy-done | bytes 8388632
  217.2 0.0 copy-start.2
  217.2 0.7 copy-done.2
  217.8 7.1 %norm.1 = (bf16[1024,4096]{1,0:T(8,128)(2,1)}, bf16[1024,4096]{1,0:T(8,128)(2,1)}) custom-call(bf16[1024,4096]{1,0:T(8,128)(2,1)S(1)} %copy-done, f32[1,1024]{1,0:T(1,128)S(1)} %copy-done.2, f32[1,4096]{1,0:T(1,128)S(1)} %bitcast.1), custom_call_target="tpu_custom_call" | custom-call | tf_op jit(solution)/shard_map/norm/pallas_call | solution.py:493
Async XLA Ops:
  0.6 213.1 %copy-start.1 = (f32[4096]{0:T(1024)S(1)}, f32[4096]{0:T(1024)}, u32[]{:S(2)}) copy-start(f32[4096]{0:T(1024)} %param.13) | copy-start | bytes 49156
  213.8 3.4 %copy-start = (bf16[1024,4096]{1,0:T(8,128)(2,1)S(1)}, bf16[1024,4096]{1,0:T(8,128)(2,1)}, u32[]{:S(2)}) copy-start(bf16[1024,4096]{1,0:T(8,128)(2,1)} %get-tuple-element.4.hid_ref) | copy-start | bytes 25165828
  217.2 0.7 copy-start.2

commit v3 on v2

--- a/solution.py
+++ b/solution.py
@@ -289,7 +289,9 @@
             device_id=partner, device_id_type=MESH)
 
     @pl.loop(0, STEPS)
-    def _(g):
+    def _(step):
+        toward = 1 - 2 * (z // 2)
+        g = lax.rem(z + NZ + toward * (step // 2), NZ) * 2 + lax.rem(step, 2)
         kcol = pl.ds(pl.multiple_of((g * per_step // group) * HD, HD), HD)
         for i, (t0, ks) in enumerate(starts):
             key = kbuf[pl.ds(ks, KT), kcol]
@@ -307,7 +309,7 @@
                 attn[pl.ds(t0, QT), hc] = (o / tot).astype(jnp.bfloat16)
         attn_copy(g).start()
         for t in (1, 2):
-            forward_chunk(t, g)
+            forward_chunk(t, step)
 
 
     def project(t, yy):
@@ -332,6 +334,10 @@
                 wload(n, 1).start()
 
             kc = pl.ds(pl.multiple_of(first * wrows, 2 * wrows), 2 * wrows)
+            g = zz * 2 + yy
+            attn_copy(g).wait_send()
+            part = attn.at[pl.ds(pl.multiple_of((1 - r) * half, half), half), kc]
+            pltpu.make_async_copy(part, part, a_recv.at[g]).wait()
 
             @pl.loop(0, nsteps)
             def _(n):
@@ -347,26 +353,18 @@
     forward_y(0)
     forward_last(1)
     forward_last(2)
+    project(0, y)
+    project(0, 1 - y)
     forward(3)
     forward(4)
     forward_last(3)
     forward_last(4)
-
-    @pl.loop(0, STEPS)
-    def _(g):
-        attn_copy(g).wait_send()
-        cols = pl.ds(pl.multiple_of(g * aw, aw), aw)
-        part = attn.at[pl.ds(pl.multiple_of((1 - r) * half, half), half), cols]
-        pltpu.make_async_copy(part, part, a_recv.at[g]).wait()
-
-    project(0, y)
     project(1, y)
     project(2, y)
     forward(5)
     forward(6)
     forward_last(5)
     forward_last(6)
-    project(0, 1 - y)
     forward_y(1)
     forward_y(2)
     project(3, y)

time: 225 us -> 227 us (level)
  no operation moved by 1% of the time
where the time goes in v3:
time: 227 us; the launch traced here: 226 us
  Pallas kernels  222 us (98%)
  local copies, waits for them, and re-layouts  4.05 us (2%)
    pallas_call x1, Pallas kernels, body_fused(): pl.pallas_call(fused_kernel, out_shape=(jax.ShapeDtypeStruct((length, wid...  215 us
    pallas_call x1, Pallas kernels, body_fused(): pl.pallas_call(norm_kernel, grid=(length // rows,), out_shape=(jax.ShapeD...  7.1 us

profile of v3, /device:TPU:1, one launch (start us, length us, event | category | flops | bytes accessed | tf_op | source)
XLA Modules:
  0.0 226.5 jit_solution(1807040825244049356)
XLA Ops:
  0.6 0.0 copy-start.1
  0.6 214.7 %fused.1 = (bf16[1024,4096]{1,0:T(8,128)(2,1)}, f32[1,1024]{1,0:T(1,128)}, bf16[16,256,4096]{2,1,0:T(8,128)(2,1)}) custom-call(bf16[512,4096]{1,0:T(8,128)(2,1)} %q_ref.1, bf16[512,512]{1,0:T(8,128)(2,1)} %k_ref.1, bf16[512,512]{1,0:T(8,128)(2,1)} %v_ref.1, s32[1,1024]{1,0:T(1,128)} %seg_row.1, bf16[256,4096]{1,0:T(8,128)(2,1)} %w_ref.1, ...), custom_call_target="tpu_custom_call" | custom-call | tf_op jit(solution)/shard_map/fused/pallas_call | solution.py:455
  215.3 0.0 copy-done.1
  215.3 0.0 copy-start
  215.3 3.4 %copy-done = bf16[1024,4096]{1,0:T(8,128)(2,1)S(1)} copy-done((bf16[1024,4096]{1,0:T(8,128)(2,1)S(1)}, bf16[1024,4096]{1,0:T(8,128)(2,1)}, u32[]{:S(2)}) %copy-start) | copy-done | bytes 8388632
  218.7 0.0 copy-start.2
  218.7 0.7 copy-done.2
  219.4 7.1 %norm.1 = (bf16[1024,4096]{1,0:T(8,128)(2,1)}, bf16[1024,4096]{1,0:T(8,128)(2,1)}) custom-call(bf16[1024,4096]{1,0:T(8,128)(2,1)S(1)} %copy-done, f32[1,1024]{1,0:T(1,128)S(1)} %copy-done.2, f32[1,4096]{1,0:T(1,128)S(1)} %bitcast.1), custom_call_target="tpu_custom_call" | custom-call | tf_op jit(solution)/shard_map/norm/pallas_call | solution.py:491
Async XLA Ops:
  0.6 214.7 %copy-start.1 = (f32[4096]{0:T(1024)S(1)}, f32[4096]{0:T(1024)}, u32[]{:S(2)}) copy-start(f32[4096]{0:T(1024)} %param.13) | copy-start | bytes 49156
  215.3 3.4 %copy-start = (bf16[1024,4096]{1,0:T(8,128)(2,1)S(1)}, bf16[1024,4096]{1,0:T(8,128)(2,1)}, u32[]{:S(2)}) copy-start(bf16[1024,4096]{1,0:T(8,128)(2,1)} %get-tuple-element.4.hid_ref) | copy-start | bytes 25165828
  218.7 0.7 copy-start.2
